TPU v7x, 128 devices: a whole 4x4x4 slice. The times are simulated.
128 devices in a mesh: expert: 16 (over x, y_hi, core), dp: 8 (over y_lo, z).
Axes of the slice: x: 4, y: 4 (y_hi: 2, y_lo: 2; y = y_hi * 2 + y_lo), z: 4, core: 2. Of those that a mesh axis runs over, the one named last changes fastest.
Arguments:
- attn_rows: bfloat16 [16384, 7168], P('dp', 'expert'), may hold values from -6 to 6
- out_grad: bfloat16 [16384, 7168], P('dp', 'expert'), may hold values from -6 to 6
- routes: int32 [16384, 8], P(('dp', 'expert')), may hold values from 0 to 255, as said below
- gates: bfloat16 [16384, 8], P(('dp', 'expert')), may hold values from 0.049804688 to 0.5
- w_gate: bfloat16 [16, 7168, 2048], P('expert', None, 'dp'), may hold values from -0.0625 to 0.0625
- w_up: bfloat16 [16, 7168, 2048], P('expert', None, 'dp'), may hold values from -0.0625 to 0.0625
- w_down: bfloat16 [16, 2048, 7168], P('expert', 'dp'), may hold values from -0.125 to 0.125
Outputs:
- grad_input: bfloat16 [16384, 7168], P('dp', 'expert')
- grad_w_gate: bfloat16 [16, 7168, 2048], P('expert', None, 'dp')
- grad_w_up: bfloat16 [16, 7168, 2048], P('expert', None, 'dp')
Inputs may be any that keep to these rules, and one draw needn't show every extreme that they name: `routes`: each row names 8 different experts. In the 128 rows of one device (aligned blocks of 128 rows) no window expert (below 16) is named by more than 6 rows; in every device's rows some window expert is named by exactly 6 rows, and one window expert is named by exactly 6 rows of every device.
All inputs are finite; a program needn't handle non-finite values.
Results may differ from a plain program's by a relative error of at most 0.0058.
Values may be sent and summed in bfloat16 or wider, within the bound.
A program may use at most 256 MiB of HBM per device.

v0:
```python
import jax
import jax.numpy as jnp
from jax import lax
from jax.sharding import PartitionSpec as P

BF = jnp.bfloat16
F32 = jnp.float32


def slot_tables(routes, gates, experts, capacity):
    matches = (routes[..., None] == jnp.arange(experts, dtype=routes.dtype)).astype(F32)
    per_token = jnp.sum(matches, axis=2)
    coef = jnp.sum(matches * gates[..., None].astype(F32), axis=2)
    tokens = routes.shape[1]
    earlier = (jnp.arange(tokens)[:, None] < jnp.arange(tokens)[None, :]).astype(BF)
    before = jnp.einsum("bse,st->bte", per_token.astype(BF), earlier, preferred_element_type=F32)
    slot = jnp.arange(capacity, dtype=F32)
    hit = (before[..., None] == slot) & (per_token[..., None] > 0)
    hit = jnp.transpose(hit, (0, 2, 3, 1))
    scaled = jnp.where(hit, jnp.transpose(coef, (0, 2, 1))[:, :, None, :], 0.0)
    return (hit.astype(BF), scaled.astype(BF))


def per_device(attn_rows, out_grad, routes, gates, w_gate, w_up, w_down):
    experts = lax.axis_size("expert")
    groups = lax.axis_size("dp")
    own = routes.shape[0]
    capacity = 3 * own // 64
    width = attn_rows.shape[1]
    packed = jnp.concatenate([routes.astype(BF), gates], axis=1)
    packed = lax.all_gather(packed, "expert", axis=0, tiled=False)
    top = routes.shape[1]
    place, scaled = slot_tables(packed[..., :top], packed[..., top:], experts, capacity)

    def dispatch(table, rows):
        rows = rows.reshape(experts, own, width)
        sent = jnp.einsum("bect,btd->ebcd", table, rows, preferred_element_type=F32).astype(BF)
        sent = sent.reshape(experts, experts * capacity, width)
        got = lax.all_to_all(sent, "expert", split_axis=0, concat_axis=0, tiled=True)
        got = jnp.transpose(got, (1, 0, 2)).reshape(experts * capacity, experts * width)
        return lax.all_gather(got, "dp", axis=0, tiled=True)

    x = dispatch(place, attn_rows)
    dy = dispatch(scaled, out_grad)
    gate_mat, up_mat, down_mat = (w_gate[0], w_up[0], w_down[0])
    rows_dims = (((1,), (1,)), ((), ()))
    first_dims = (((0,), (0,)), ((), ()))
    g = jnp.dot(x, gate_mat, preferred_element_type=F32)
    u = jnp.dot(x, up_mat, preferred_element_type=F32)
    gh = lax.dot_general(dy, down_mat, rows_dims, preferred_element_type=F32)
    s = jax.nn.sigmoid(g)
    dg = (gh * u * s * (1.0 + g * (1.0 - s))).astype(BF)
    du = (gh * (g * s)).astype(BF)
    part = lax.dot_general(dg, gate_mat, rows_dims, preferred_element_type=F32)
    part = (part + lax.dot_general(du, up_mat, rows_dims, preferred_element_type=F32)).astype(BF)
    back = lax.psum_scatter(part, "dp", scatter_dimension=0, tiled=True)
    g_gate = lax.dot_general(x, dg, first_dims, preferred_element_type=F32).astype(BF)
    g_up = lax.dot_general(x, du, first_dims, preferred_element_type=F32).astype(BF)
    back = back.reshape(experts * capacity, experts, width)
    back = jnp.transpose(back, (1, 0, 2))
    back = lax.all_to_all(back, "expert", split_axis=0, concat_axis=0, tiled=True)
    back = back.reshape(experts, experts, capacity, width)
    grad_input = jnp.einsum("bect,ebcd->btd", place, back, preferred_element_type=F32).astype(BF)
    return (grad_input.reshape(experts * own, width), g_gate[None], g_up[None])


def solution(mesh):
    return jax.shard_map(
        per_device,
        mesh=mesh,
        in_specs=(
            P("dp", "expert"),
            P("dp", "expert"),
            P(("dp", "expert"), None),
            P(("dp", "expert"), None),
            P("expert", None, "dp"),
            P("expert", None, "dp"),
            P("expert", "dp", None),
        ),
        out_specs=(P("dp", "expert"), P("expert", None, "dp"), P("expert", None, "dp")),
        check_vma=False,
    )
```

profile of v0, /device:TPU:1, one launch (start us, length us, event | category | flops | bytes accessed | tf_op | source)
XLA Modules:
  0.0 514.2 jit_solution(15024579949341409885)
XLA Ops:
  7.2 0.0 all-gather.6.cloned.1.call-start
  7.2 0.7 convert_element_type.48
  7.9 0.7 pad_maximum_fusion
  8.6 25.8 %all-gather = bf16[2048,16]{0,1:T(8,128)(2,1)S(1)} all-gather(bf16[128,16]{0,1:T(8,128)(2,1)S(1)} %pad_maximum_fusion), channel_id=2, replica_groups=mesh['expert'=16,'dp'=8] {'expert'}, dimensions={0}, use_global_device_ids=true | all-gather | bytes 69632 | tf_op jit(solution)/shard_map/all_gather | solution.py:31
  34.4 0.8 convert_reduce_fusion
  35.3 0.0 copy-start.3
  35.3 0.1 fusion.45
  35.5 2.0 copy.62
  37.5 0.9 fusion.18
  38.4 0.0 copy-done.3
  38.4 0.9 copy.45
  39.3 25.1 %all_to_all.15 = bf16[16,96,448]{2,1,0:T(8,128)(2,1)S(1)} all-to-all(bf16[16,96,448]{2,1,0:T(8,128)(2,1)S(1)} %copy.45), channel_id=1, replica_groups=mesh['expert'=16,'dp'=8] {'expert'}, dimensions={0} | all-to-all | bytes 2752512 | tf_op jit(solution)/shard_map/all_to_all | solution.py:39
  64.4 0.0 copy-start.2
  64.4 0.9 copy.46
  65.3 2.7 reshape.47
  68.0 0.0 copy-start.4
  68.0 0.0 copy-start.5
  68.0 0.0 all-gather.6.cloned.1.call-update
  68.0 0.0 all-gather.4.cloned.1.call-start
  68.0 0.0 copy-done.2
  68.0 0.5 copy.61
  68.6 0.1 copy-done.4
  68.7 0.1 copy-done.5
  68.8 0.9 fusion.15
  69.7 0.9 copy.42
  70.6 29.3 %all_to_all.16 = bf16[16,96,448]{2,1,0:T(8,128)(2,1)S(1)} all-to-all(bf16[16,96,448]{2,1,0:T(8,128)(2,1)S(1)} %copy.42), channel_id=1, replica_groups=mesh['expert'=16,'dp'=8] {'expert'}, dimensions={0} | all-to-all | bytes 2752512 | tf_op jit(solution)/shard_map/all_to_all | solution.py:39
  99.9 0.9 copy.43
  100.8 2.7 reshape.44
  103.5 0.0 all-gather.4.cloned.1.call-update
  103.5 0.2 reduce-scatter.2.cloned.1.call-start
  103.7 96.4 %all-gather.6.cloned.1.call-done = bf16[768,7168]{1,0:T(8,128)(2,1)} async-done(((bf16[96,7168]{1,0:T(8,128)(2,1)}), bf16[768,7168]{1,0:T(8,128)(2,1)}) %all-gather.6.cloned.1.call-update) | async-done | bytes 11010064 | tf_op jit(solution)/shard_map/all_gather | solution.py:41
  200.1 6.9 %fusion.4 = f32[768,256]{1,0:T(8,128)S(1)} fusion(bf16[768,7168]{1,0:T(8,128)(2,1)} %all-gather.6.cloned.1.call-done, bf16[1,7168,256]{2,1,0:T(8,128)(2,1)} %param.11), kind=kOutput, calls=%fused_computation.8 | convolution fusion | flops 2818572288 | bytes 15466496 | tf_op jit(solution)/shard_map/dot_general | solution.py:48
  207.0 0.0 copy-start.7
  207.0 110.1 %all-gather.4.cloned.1.call-done = bf16[768,7168]{1,0:T(8,128)(2,1)} async-done(((bf16[96,7168]{1,0:T(8,128)(2,1)}), bf16[768,7168]{1,0:T(8,128)(2,1)}) %all-gather.4.cloned.1.call-update) | async-done | bytes 11010064 | tf_op jit(solution)/shard_map/all_gather | solution.py:41
  317.2 0.0 copy-start
  317.2 0.0 copy-start.6
  317.2 7.1 %multiply_convert_fusion = (bf16[768,256]{1,0:T(8,128)(2,1)S(1)}, f32[768,256]{1,0:T(8,128)S(1)}) fusion(f32[768,256]{1,0:T(8,128)S(1)} %fusion.4, bf16[768,7168]{1,0:T(8,128)(2,1)} %all-gather.4.cloned.1.call-done, bf16[1,256,7168]{2,1,0:T(8,128)(2,1)} %param.13), kind=kOutput, calls=%fused_computation.30 | convolution fusion | flops 2819751936 | bytes 16646144 | tf_op jit(solution)/shard_map/dot_general | solution.py:50
  324.3 0.0 copy-done.7
  324.3 0.0 copy-done
  324.3 2.4 copy-done.6
  326.6 0.0 copy-start.1
  326.6 4.5 fusion.31
  331.1 0.0 copy-done.1
  331.1 9.1 %fusion.2 = f32[768,7168]{1,0:T(8,128)} fusion(bf16[768,256]{1,0:T(8,128)(2,1)S(1)} %fusion.31, bf16[1,7168,256]{2,1,0:T(8,128)(2,1)S(1)} %copy-done.1), kind=kOutput, calls=%fused_computation.6 | convolution fusion | flops 2818572288 | bytes 26083328 | tf_op jit(solution)/shard_map/dot_general | solution.py:54
  340.2 12.6 %add_convert_fusion = bf16[768,7168]{1,0:T(8,128)(2,1)} fusion(f32[768,7168]{1,0:T(8,128)} %fusion.2, bf16[768,256]{1,0:T(8,128)(2,1)S(1)} %get-tuple-element.7, bf16[1,7168,256]{2,1,0:T(8,128)(2,1)S(1)} %copy-done), kind=kOutput, calls=%fused_computation | convolution fusion | flops 2829582336 | bytes 37093376 | tf_op jit(solution)/shard_map/dot_general | solution.py:55
  352.7 0.0 reduce-scatter.2.cloned.1.call-update
  352.8 116.6 %reduce-scatter.2.cloned.1.call-done = bf16[96,7168]{1,0:T(8,128)(2,1)} async-done(((bf16[768,7168]{1,0:T(8,128)(2,1)}), bf16[96,7168]{1,0:T(8,128)(2,1)}) %reduce-scatter.2.cloned.1.call-update) | async-done | bytes 1376272 | tf_op jit(solution)/shard_map/reduce_scatter | solution.py:56
  469.3 3.1 reshape.48
  472.5 2.0 copy.75
  474.5 7.1 %all-to-all-start.2 = ((bf16[16,96,448]{2,1,0:T(8,128)(2,1)}), bf16[16,96,448]{2,1,0:T(8,128)(2,1)S(1)}, u32[]{:S(2)}, u32[]{:S(2)}) async-start(bf16[16,96,448]{2,1,0:T(8,128)(2,1)} %bitcast.80), calls=%async_computation.3 | async-start | bytes 3145728 | tf_op jit(solution)/shard_map/all_to_all | solution.py:61
  481.6 9.1 %fusion = bf16[1,7168,256]{2,1,0:T(8,128)(2,1)} fusion(bf16[768,7168]{1,0:T(8,128)(2,1)} %all-gather.6.cloned.1.call-done, bf16[768,256]{1,0:T(8,128)(2,1)S(1)} %fusion.31), kind=kOutput, calls=%fused_computation.3 | convolution fusion | flops 2820407296 | bytes 15073280 | tf_op jit(solution)/shard_map/dot_general | solution.py:57
  490.7 9.1 %fusion.1 = bf16[1,7168,256]{2,1,0:T(8,128)(2,1)} fusion(bf16[768,7168]{1,0:T(8,128)(2,1)} %all-gather.6.cloned.1.call-done, bf16[768,256]{1,0:T(8,128)(2,1)S(1)} %get-tuple-element.7), kind=kOutput, calls=%fused_computation.4 | convolution fusion | flops 2820407296 | bytes 15073280 | tf_op jit(solution)/shard_map/dot_general | solution.py:58
  499.8 4.6 all-to-all-done.2
  504.3 0.9 copy.48
  505.2 0.8 fusion.21
  506.0 1.7 copy.74
  (5 shorter events, 0.1 us)
Async XLA Ops:
  7.2 193.0 %all-gather.6.cloned.1.call-start = ((), (), s32[]{:S(2)}) async-start(), calls=%async_computation.5 | async-start | bytes 12386304 | tf_op jit(solution)/shard_map/all_gather | solution.py:41
  35.3 3.1 copy-start.3
  64.4 3.6 copy-start.2
  68.0 0.8 copy-start.4
  68.0 0.9 copy-start.5
  68.0 249.2 %all-gather.4.cloned.1.call-start = ((), (), s32[]{:S(2)}) async-start(), calls=%async_computation.4 | async-start | bytes 12386304 | tf_op jit(solution)/shard_map/all_gather | solution.py:41
  103.5 365.8 %reduce-scatter.2.cloned.1.call-start = ((), (), s32[]{:S(2)}) async-start(), calls=%async_computation.6 | async-start | bytes 12386304 | tf_op jit(solution)/shard_map/reduce_scatter | solution.py:56
  207.0 117.3 %copy-start.7 = (f32[768,256]{1,0:T(8,128)}, f32[768,256]{1,0:T(8,128)S(1)}, u32[]{:S(2)}) copy-start(f32[768,256]{1,0:T(8,128)S(1)} %fusion.4) | copy-start | bytes 2359300
  317.2 7.1 %copy-start = (bf16[1,7168,256]{2,1,0:T(8,128)(2,1)S(1)}, bf16[1,7168,256]{2,1,0:T(8,128)(2,1)}, u32[]{:S(2)}) copy-start(bf16[1,7168,256]{2,1,0:T(8,128)(2,1)} %param.12) | copy-start | bytes 11010052
  317.2 9.5 %copy-start.6 = (bf16[768,7168]{1,0:T(8,128)(2,1)S(1)}, bf16[768,7168]{1,0:T(8,128)(2,1)}, u32[]{:S(2)}) copy-start(bf16[768,7168]{1,0:T(8,128)(2,1)} %all-gather.6.cloned.1.call-done) | copy-start | bytes 33030148
  326.6 4.5 copy-start.1
  474.5 29.8 %all-to-all-start.2 = ((bf16[16,96,448]{2,1,0:T(8,128)(2,1)}), bf16[16,96,448]{2,1,0:T(8,128)(2,1)S(1)}, u32[]{:S(2)}, u32[]{:S(2)}) async-start(bf16[16,96,448]{2,1,0:T(8,128)(2,1)} %bitcast.80), calls=%async_computation.3 | async-start | bytes 3145728 | tf_op jit(solution)/shard_map/all_to_all | solution.py:61
Sparse Core Ops, SparseCore 0:
  68.1 131.9 all-gather.5
  202.3 114.7 all-gather.3
  352.9 116.4 reduce-scatter.1
where the time goes:
time: 515 us; the launch traced here: 514 us
  waiting for transfers between devices  328 us (64%)
  blocking collectives  80.2 us (16%)
  matrix products  60.9 us (12%)
  local copies, waits for them, and re-layouts  21.8 us (4%)
  between operations  13.9 us (3%)
  starting transfers between devices  7.45 us (1%)
    all_gather x2, waiting for transfers between devices, dispatch(): return lax.all_gather(got, 'dp', axis=0, tiled=True)  207 us
    reduce_scatter x1, waiting for transfers between devices, per_device(): back = lax.psum_scatter(part, 'dp', scatter_dimension=0, tiled=True)  117 us
    all_to_all x2, blocking collectives, dispatch(): lax.all_to_all(sent, 'expert', split_axis=0, concat_axis=0, tiled=True)  54.4 us
    all_gather x1, blocking collectives, per_device(): packed = lax.all_gather(packed, 'expert', axis=0, tiled=False)  25.8 us
    dot_general x1, matrix products, per_device(): lax.dot_general(du, up_mat, rows_dims, preferred_element_type=F32)  12.6 us
  transfers between devices with their start and end apart: 4, of which 4 were waited for; matrix products, arithmetic and copies ran while one was open for 6% of the time, Pallas kernels for 0%

commit v1 on v0

--- a/solution.py
+++ b/solution.py
@@ -2,6 +2,7 @@
 import jax.numpy as jnp
 from jax import lax
 from jax.sharding import PartitionSpec as P
+from jax.lax import all_to_all, axis_size
 
 BF = jnp.bfloat16
 F32 = jnp.float32
@@ -38,7 +39,9 @@
         sent = sent.reshape(experts, experts * capacity, width)
         got = lax.all_to_all(sent, "expert", split_axis=0, concat_axis=0, tiled=True)
         got = jnp.transpose(got, (1, 0, 2)).reshape(experts * capacity, experts * width)
-        return lax.all_gather(got, "dp", axis=0, tiled=True)
+        return jnp.concatenate(
+            all_to_all(jnp.stack([got for _ in range(axis_size("dp"))]), "dp", 0, 0), axis=0
+        )
 
     x = dispatch(place, attn_rows)
     dy = dispatch(scaled, out_grad)

time: 515 us -> 559 us (1.085)
  waiting for transfers between devices: 328 us -> 389 us
  blocking collectives: 80.2 us -> 25.8 us
  starting transfers between devices: 7.45 us -> 26.2 us
  local copies, waits for them, and re-layouts: 21.8 us -> 34.5 us
  matrix products: 60.9 us -> 66.9 us
    all_to_all x0 -> x4, waiting for transfers between devices: none -> 268 us  [the longest x2 233 us: dispatch(): all_to_all(jnp.stack([got for _ in range(axis_size('dp'))]), 'dp', 0, 0)]
    all_gather x2 -> x0, waiting for transfers between devices: 207 us -> none  [dispatch(): return lax.all_gather(got, 'dp', axis=0, tiled=True)]
    all_to_all x2 -> x0, blocking collectives: 54.4 us -> none  [dispatch(): lax.all_to_all(sent, 'expert', split_axis=0, concat_axis=0, tiled=True)]
    all_to_all x0 -> x4, starting transfers between devices: none -> 18.8 us  [the longest x2 10.4 us: dispatch(): all_to_all(jnp.stack([got for _ in range(axis_size('dp'))]), 'dp', 0, 0)]
    another operation x0 -> x4, local copies, waits for them, and re-layouts: none -> 15.8 us  [dispatch(): jnp.stack([got for _ in range(axis_size('dp'))])]
  transfers between devices with their start and end apart: 4 -> 6, of which waited for: 4 -> 6; matrix products, arithmetic and copies ran while one was open for 6% -> 7% of each run, Pallas kernels for 0% -> 0%
where the time goes in v1:
time: 559 us; the launch traced here: 558 us
  waiting for transfers between devices  389 us (70%)
  matrix products  66.9 us (12%)
  local copies, waits for them, and re-layouts  34.5 us (6%)
  starting transfers between devices  26.2 us (5%)
  blocking collectives  25.8 us (5%)
  between operations  14.2 us (3%)
    all_to_all x2, waiting for transfers between devices, dispatch(): all_to_all(jnp.stack([got for _ in range(axis_size('dp'))]), 'dp', 0, 0)  233 us
    reduce_scatter x1, waiting for transfers between devices, per_device(): back = lax.psum_scatter(part, 'dp', scatter_dimension=0, tiled=True)  116 us
    all_to_all x2, waiting for transfers between devices, dispatch(): lax.all_to_all(sent, 'expert', split_axis=0, concat_axis=0, tiled=True)  35.5 us
    all_gather x1, blocking collectives, per_device(): packed = lax.all_gather(packed, 'expert', axis=0, tiled=False)  25.8 us
    another operation x4, local copies, waits for them, and re-layouts, dispatch(): jnp.stack([got for _ in range(axis_size('dp'))])  15.8 us
    dot_general x1, matrix products, per_device(): lax.dot_general(du, up_mat, rows_dims, preferred_element_type=F32)  11.8 us
  transfers between devices with their start and end apart: 6, of which 6 were waited for; matrix products, arithmetic and copies ran while one was open for 7% of the time, Pallas kernels for 0%

profile of v1, /device:TPU:1, one launch (start us, length us, event | category | flops | bytes accessed | tf_op | source)
XLA Modules:
  0.0 557.9 jit_solution(6037718442242459409)
XLA Ops:
  7.2 0.7 convert_element_type.48
  7.9 0.7 pad_maximum_fusion
  8.5 25.8 %all-gather = bf16[2048,16]{0,1:T(8,128)(2,1)S(1)} all-gather(bf16[128,16]{0,1:T(8,128)(2,1)S(1)} %pad_maximum_fusion), channel_id=2, replica_groups=mesh['expert'=16,'dp'=8] {'expert'}, dimensions={0}, use_global_device_ids=true | all-gather | bytes 69632 | tf_op jit(solution)/shard_map/all_gather | solution.py:32
  34.4 0.2 convert_reduce_fusion
  34.6 0.1 fusion.45
  34.8 2.0 copy.62
  36.8 0.9 fusion.18
  37.7 2.0 copy.45
  39.8 3.7 all-to-all-start.2
  43.4 2.0 copy.61
  45.4 0.9 fusion.15
  46.4 2.0 copy.42
  48.4 17.8 %all-to-all-done.2 = bf16[16,96,448]{2,1,0:T(8,128)(2,1)S(1)} async-done(((bf16[16,96,448]{2,1,0:T(8,128)(2,1)}), bf16[16,96,448]{2,1,0:T(8,128)(2,1)S(1)}, u32[]{:S(2)}, u32[]{:S(2)}) %all-to-all-start.2) | async-done | bytes 1376288 | tf_op jit(solution)/shard_map/all_to_all | solution.py:40
  66.2 4.8 all-to-all-start
  71.0 2.0 copy.46
  73.0 3.0 stack_reshape.5
  76.0 17.7 %all-to-all-done = bf16[16,96,448]{2,1,0:T(8,128)(2,1)S(1)} async-done(((bf16[16,96,448]{2,1,0:T(8,128)(2,1)}), bf16[16,96,448]{2,1,0:T(8,128)(2,1)S(1)}, u32[]{:S(2)}, u32[]{:S(2)}) %all-to-all-start) | async-done | bytes 1376288 | tf_op jit(solution)/shard_map/all_to_all | solution.py:40
  93.7 5.5 stack.7
  99.2 5.2 all-to-all-start.3
  104.4 0.9 copy.43
  105.3 1.8 stack_reshape.4
  107.2 120.3 %all-to-all-done.3 = bf16[8,96,7168]{2,1,0:T(8,128)(2,1)} async-done(((bf16[8,96,7168]{2,1,0:T(8,128)(2,1)}), bf16[8,96,7168]{2,1,0:T(8,128)(2,1)}, u32[]{:S(2)}, u32[]{:S(2)}) %all-to-all-start.3) | async-done | bytes 11010080 | tf_op jit(solution)/shard_map/all_to_all | solution.py:43
  227.4 5.4 stack.6
  232.8 5.2 all-to-all-start.1
  238.0 0.2 reduce-scatter.2.cloned.1.call-start
  238.2 9.1 %fusion.4 = f32[768,256]{1,0:T(8,128)} fusion(bf16[768,7168]{1,0:T(8,128)(2,1)} %bitcast.13, bf16[1,7168,256]{2,1,0:T(8,128)(2,1)} %param.11), kind=kOutput, calls=%fused_computation.8 | convolution fusion | flops 2818572288 | bytes 15466496 | tf_op jit(solution)/shard_map/dot_general | solution.py:51
  247.3 112.4 %all-to-all-done.1 = bf16[8,96,7168]{2,1,0:T(8,128)(2,1)} async-done(((bf16[8,96,7168]{2,1,0:T(8,128)(2,1)}), bf16[8,96,7168]{2,1,0:T(8,128)(2,1)}, u32[]{:S(2)}, u32[]{:S(2)}) %all-to-all-start.1) | async-done | bytes 11010080 | tf_op jit(solution)/shard_map/all_to_all | solution.py:43
  359.7 0.0 copy-start
  359.7 0.0 copy-start.2
  359.7 8.6 %multiply_convert_fusion = (bf16[768,256]{1,0:T(8,128)(2,1)S(1)}, f32[768,256]{1,0:T(8,128)S(1)}) fusion(f32[768,256]{1,0:T(8,128)} %fusion.4, bf16[768,7168]{1,0:T(8,128)(2,1)} %bitcast.7, bf16[1,256,7168]{2,1,0:T(8,128)(2,1)} %param.13), kind=kOutput, calls=%fused_computation.30 | convolution fusion | flops 2819751936 | bytes 16646144 | tf_op jit(solution)/shard_map/dot_general | solution.py:53
  368.3 0.0 copy-done
  368.3 0.0 copy-done.2
  368.3 0.0 copy-start.1
  368.3 7.4 %fusion.31 = bf16[768,256]{1,0:T(8,128)(2,1)S(1)} fusion(f32[768,256]{1,0:T(8,128)S(1)} %get-tuple-element.8, bf16[768,7168]{1,0:T(8,128)(2,1)} %bitcast.13, bf16[1,7168,256]{2,1,0:T(8,128)(2,1)S(1)} %copy-done, f32[768,256]{1,0:T(8,128)S(1)} %copy-done.2), kind=kOutput, calls=%fused_computation.27 | convolution fusion | flops 2820538368 | bytes 16646144 | tf_op jit(solution)/shard_map/dot_general | solution.py:52
  375.7 0.0 copy-done.1
  375.7 9.2 %fusion.2 = f32[768,7168]{1,0:T(8,128)} fusion(bf16[768,256]{1,0:T(8,128)(2,1)S(1)} %fusion.31, bf16[1,7168,256]{2,1,0:T(8,128)(2,1)S(1)} %copy-done.1), kind=kOutput, calls=%fused_computation.6 | convolution fusion | flops 2818572288 | bytes 26083328 | tf_op jit(solution)/shard_map/dot_general | solution.py:57
  384.9 11.8 %add_convert_fusion = bf16[768,7168]{1,0:T(8,128)(2,1)} fusion(f32[768,7168]{1,0:T(8,128)} %fusion.2, bf16[768,256]{1,0:T(8,128)(2,1)S(1)} %get-tuple-element.7, bf16[1,7168,256]{2,1,0:T(8,128)(2,1)S(1)} %copy-done), kind=kOutput, calls=%fused_computation | convolution fusion | flops 2829582336 | bytes 37093376 | tf_op jit(solution)/shard_map/dot_general | solution.py:58
  396.7 0.0 reduce-scatter.2.cloned.1.call-update
  396.7 115.9 %reduce-scatter.2.cloned.1.call-done = bf16[96,7168]{1,0:T(8,128)(2,1)} async-done(((bf16[768,7168]{1,0:T(8,128)(2,1)}), bf16[96,7168]{1,0:T(8,128)(2,1)}) %reduce-scatter.2.cloned.1.call-update) | async-done | bytes 1376272 | tf_op jit(solution)/shard_map/reduce_scatter | solution.py:59
  512.7 3.1 reshape.52
  515.8 2.0 copy.75
  517.8 7.2 %all-to-all-start.4 = ((bf16[16,96,448]{2,1,0:T(8,128)(2,1)}), bf16[16,96,448]{2,1,0:T(8,128)(2,1)S(1)}, u32[]{:S(2)}, u32[]{:S(2)}) async-start(bf16[16,96,448]{2,1,0:T(8,128)(2,1)} %bitcast.82), calls=%async_computation.5 | async-start | bytes 3145728 | tf_op jit(solution)/shard_map/all_to_all | solution.py:64
  525.0 9.1 %fusion = bf16[1,7168,256]{2,1,0:T(8,128)(2,1)} fusion(bf16[768,7168]{1,0:T(8,128)(2,1)} %bitcast.13, bf16[768,256]{1,0:T(8,128)(2,1)S(1)} %fusion.31), kind=kOutput, calls=%fused_computation.3 | convolution fusion | flops 2820407296 | bytes 15073280 | tf_op jit(solution)/shard_map/dot_general | solution.py:60
  534.1 9.1 %fusion.1 = bf16[1,7168,256]{2,1,0:T(8,128)(2,1)} fusion(bf16[768,7168]{1,0:T(8,128)(2,1)} %bitcast.13, bf16[768,256]{1,0:T(8,128)(2,1)S(1)} %get-tuple-element.7), kind=kOutput, calls=%fused_computation.4 | convolution fusion | flops 2820407296 | bytes 15073280 | tf_op jit(solution)/shard_map/dot_general | solution.py:61
  543.1 4.5 all-to-all-done.4
  547.7 0.9 copy.48
  548.5 0.8 fusion.21
  549.3 1.7 copy.74
  (5 shorter events, 0.1 us)
Async XLA Ops:
  39.8 26.4 %all-to-all-start.2 = ((bf16[16,96,448]{2,1,0:T(8,128)(2,1)}), bf16[16,96,448]{2,1,0:T(8,128)(2,1)S(1)}, u32[]{:S(2)}, u32[]{:S(2)}) async-start(bf16[16,96,448]{2,1,0:T(8,128)(2,1)} %copy.45), calls=%async_computation.2 | async-start | bytes 3145728 | tf_op jit(solution)/shard_map/all_to_all | solution.py:40
  66.2 27.5 %all-to-all-start = ((bf16[16,96,448]{2,1,0:T(8,128)(2,1)}), bf16[16,96,448]{2,1,0:T(8,128)(2,1)S(1)}, u32[]{:S(2)}, u32[]{:S(2)}) async-start(bf16[16,96,448]{2,1,0:T(8,128)(2,1)} %copy.42), calls=%async_computation | async-start | bytes 3145728 | tf_op jit(solution)/shard_map/all_to_all | solution.py:40
  99.2 128.2 %all-to-all-start.3 = ((bf16[8,96,7168]{2,1,0:T(8,128)(2,1)}), bf16[8,96,7168]{2,1,0:T(8,128)(2,1)}, u32[]{:S(2)}, u32[]{:S(2)}) async-start(bf16[8,96,7168]{2,1,0:T(8,128)(2,1)} %stack.7), calls=%async_computation.3 | async-start | bytes 22020096 | tf_op jit(solution)/shard_map/all_to_all | solution.py:43
  232.8 126.9 %all-to-all-start.1 = ((bf16[8,96,7168]{2,1,0:T(8,128)(2,1)}), bf16[8,96,7168]{2,1,0:T(8,128)(2,1)}, u32[]{:S(2)}, u32[]{:S(2)}) async-start(bf16[8,96,7168]{2,1,0:T(8,128)(2,1)} %stack.6), calls=%async_computation.1 | async-start | bytes 22020096 | tf_op jit(solution)/shard_map/all_to_all | solution.py:43
  238.0 274.7 %reduce-scatter.2.cloned.1.call-start = ((), (), s32[]{:S(2)}) async-start(), calls=%async_computation.6 | async-start | bytes 12386304 | tf_op jit(solution)/shard_map/reduce_scatter | solution.py:59
  359.7 8.6 %copy-start = (bf16[1,7168,256]{2,1,0:T(8,128)(2,1)S(1)}, bf16[1,7168,256]{2,1,0:T(8,128)(2,1)}, u32[]{:S(2)}) copy-start(bf16[1,7168,256]{2,1,0:T(8,128)(2,1)} %param.12) | copy-start | bytes 11010052
  359.7 8.6 %copy-start.2 = (f32[768,256]{1,0:T(8,128)S(1)}, f32[768,256]{1,0:T(8,128)}, u32[]{:S(2)}) copy-start(f32[768,256]{1,0:T(8,128)} %fusion.4) | copy-start | bytes 2359300
  368.3 7.5 %copy-start.1 = (bf16[1,7168,256]{2,1,0:T(8,128)(2,1)S(1)}, bf16[1,7168,256]{2,1,0:T(8,128)(2,1)}, u32[]{:S(2)}) copy-start(bf16[1,7168,256]{2,1,0:T(8,128)(2,1)} %param.11) | copy-start | bytes 11010052
  517.8 29.9 %all-to-all-start.4 = ((bf16[16,96,448]{2,1,0:T(8,128)(2,1)}), bf16[16,96,448]{2,1,0:T(8,128)(2,1)S(1)}, u32[]{:S(2)}, u32[]{:S(2)}) async-start(bf16[16,96,448]{2,1,0:T(8,128)(2,1)} %bitcast.82), calls=%async_computation.5 | async-start | bytes 3145728 | tf_op jit(solution)/shard_map/all_to_all | solution.py:64
Sparse Core Ops, SparseCore 0:
  396.9 115.7 reduce-scatter.1
